TPU v7x, 768 devices: a whole 4x8x12 slice. The times are simulated.
768 devices in a mesh: ka: 48 (over z, x_lo, core), ba: 16 (over y, x_hi).
Axes of the slice: x: 4 (x_hi: 2, x_lo: 2; x = x_hi * 2 + x_lo), y: 8, z: 12, core: 2. Of those that a mesh axis runs over, the one named last changes fastest.
Arguments:
- orbitals: bfloat16 [48, 16, 2, 32768], P('ka', 'ba'), may hold values from -6 to 6
- kpoint_coords: int32 [48, 3], replicated, may hold values from 0 to 3
Outputs:
- exchange_field: float32 [48, 16, 2, 32768], P('ka', 'ba')
All inputs are finite; a program needn't handle non-finite values.
Results may differ from a plain program's by a relative error of at most 0.0074.
Values may be sent and summed in bfloat16 or wider, within the bound.
A program may use at most 32 MiB of HBM per device.

v0:
```python
import math

import jax
import jax.numpy as jnp
from jax import lax
from jax.sharding import PartitionSpec as P

GRID = 32


def shifted(value, axis, steps):
    count = lax.axis_size(axis)
    pairs = [(source, (source + steps) % count) for source in range(count)]
    return lax.ppermute(value, axis, pairs)


def partner(value, axis, apart):
    mask = 2**apart
    pairs = [(source, source ^ mask) for source in range(lax.axis_size(axis))]
    return lax.ppermute(value, axis, pairs)


def wave_tables(grid, sign):
    index = jnp.arange(grid, dtype=jnp.int32)
    phase = index[:, None] * index[None, :] % grid
    angle = phase.astype(jnp.float32) * (2.0 * math.pi / grid)
    cosine = jnp.cos(angle)
    sine = sign * jnp.sin(angle)
    table = jnp.stack([jnp.stack([cosine, sine]), jnp.stack([-sine, cosine])])
    return table.astype(jnp.bfloat16)


def one_pass(field, table, grid):
    count = field.shape[0]
    shaped = field.reshape(count, 2, grid * grid, grid)
    result = jnp.einsum("pcme,dcfe->pdfm", shaped, table, preferred_element_type=jnp.float32)
    return result.reshape(count, 2, grid**3)


def transform(field, table, grid):
    first = one_pass(field, table, grid).astype(jnp.bfloat16)
    second = one_pass(first, table, grid).astype(jnp.bfloat16)
    return one_pass(second, table, grid)


def coulomb_kernel(offset, grid):
    index = jnp.arange(grid, dtype=jnp.int32)
    signed = jnp.where(index < grid // 2, index, index - grid).astype(jnp.float32)
    along_x = signed[:, None, None] + offset[0]
    along_y = signed[None, :, None] + offset[1]
    along_z = signed[None, None, :] + offset[2]
    square = along_x * along_x + along_y * along_y + along_z * along_z
    return (32.0 / grid**3 / (square + 0.25)).reshape(grid**3)


def pair_density(former, latter):
    f_real = former[..., :, None, 0, :].astype(jnp.float32)
    f_imag = former[..., :, None, 1, :].astype(jnp.float32)
    l_real = latter[..., None, :, 0, :].astype(jnp.float32)
    l_imag = latter[..., None, :, 1, :].astype(jnp.float32)
    real = l_real * f_real + l_imag * f_imag
    imag = l_real * f_imag - l_imag * f_real
    return jnp.stack([real, imag], axis=-2).astype(jnp.bfloat16)


def coulomb_fields(former, latter, kernel, forward, inverse):
    density = pair_density(former, latter)
    flat = density.reshape(-1, 2, GRID**3)
    spectrum = transform(flat, forward, GRID)
    screened = (spectrum * kernel).astype(jnp.bfloat16)
    return transform(screened, inverse, GRID).reshape(density.shape)


def apply_fields(fields, latter):
    w_real = fields[..., 0, :]
    w_imag = fields[..., 1, :]
    l_real = latter[..., None, :, 0, :].astype(jnp.float32)
    l_imag = latter[..., None, :, 1, :].astype(jnp.float32)
    real = -jnp.sum(l_real * w_real - l_imag * w_imag, axis=-2)
    imag = -jnp.sum(l_real * w_imag + l_imag * w_real, axis=-2)
    return jnp.stack([real, imag], axis=-2)


def back_fields(fields, former):
    w_real = fields[..., 0, :]
    w_imag = fields[..., 1, :]
    f_real = former[..., :, None, 0, :].astype(jnp.float32)
    f_imag = former[..., :, None, 1, :].astype(jnp.float32)
    real = -jnp.sum(f_real * w_real + f_imag * w_imag, axis=-3)
    imag = -jnp.sum(f_imag * w_real - f_real * w_imag, axis=-3)
    return jnp.stack([real, imag], axis=-2)


def fields_all(formers, latters, kernel, forward, inverse):
    return [
        coulomb_fields(former[None], latter[None], kernel, forward, inverse)[0]
        for former, latter in zip(formers, latters)
    ]


def per_device(orbitals, kpoint_coords):
    own = orbitals[0]
    kpoints = lax.axis_size("ka")
    offset_steps = kpoints // 4
    matches = min(3, lax.axis_size("ba") // 4 + 1)
    forward = wave_tables(GRID, 1.0)
    inverse = wave_tables(GRID, -1.0)
    coords = kpoint_coords.astype(jnp.float32)
    rows_all = jnp.arange(kpoints, dtype=jnp.int32)
    here = lax.axis_index("ka")

    def coord_of(position):
        picked = (rows_all == position).astype(jnp.float32)
        return jnp.dot(picked, coords, precision=lax.Precision.HIGHEST)

    source = (here - offset_steps) % kpoints
    kernel = coulomb_kernel((coord_of(here) - coord_of(source)) / 4.0, GRID)
    received = shifted(own, "ka", offset_steps)
    partners = [partner(received, "ba", matching) for matching in range(matches)]
    fields = fields_all([own] * matches, partners, kernel, forward, inverse)
    total = jnp.zeros(own.shape, jnp.float32)
    for matching in range(matches):
        total = total + apply_fields(fields[matching], partners[matching])
    outgoing = [
        back_fields(fields[matching], own).astype(jnp.bfloat16) for matching in range(matches)
    ]
    summed = jnp.zeros(own.shape, jnp.float32)
    for matching in range(matches):
        arrived = partner(outgoing[matching], "ba", matching)
        summed = summed + arrived.astype(jnp.float32)
    total = total + shifted(summed, "ka", -offset_steps)
    return total[None]


def solution(mesh):
    return jax.shard_map(
        per_device,
        mesh=mesh,
        in_specs=(P("ka", "ba", None, None), P()),
        out_specs=P("ka", "ba", None, None),
        check_vma=False,
    )
```

profile of v0, /device:TPU:1, one launch (start us, length us, event | category | flops | bytes accessed | tf_op | source)
XLA Modules:
  0.0 93.4 jit_solution(2225463952021821871)
XLA Ops:
  0.0 8.4 %collective-permute-start = (bf16[1,2,32768]{2,1,0:T(2,128)(2,1)}, bf16[1,2,32768]{2,1,0:T(2,128)(2,1)S(1)}, u32[]{:S(2)}, u32[]{:S(2)}) collective-permute-start(bf16[1,2,32768]{2,1,0:T(2,128)(2,1)} %bitcast.223), channel_id=1, source_target_pairs={{0,192},{16,208},{32,224},{48,240},{64,256},{80,272},{96,288},{112... | collective-permute-start | bytes 393224 | tf_op jit(solution)/shard_map/ppermute | solution.py:14
  8.5 0.7 copy-done.1
  9.4 0.7 fusion.70
  10.1 0.6 add_multiply_fusion
  10.7 1.3 %add_multiply_fusion.1 = (f32[32]{0:T(128)S(1)}, f32[32]{0:T(128)S(1)}) fusion(f32[]{:T(128)} %bitcast.20, f32[]{:T(128)} %bitcast.19), kind=kLoop, calls=%fused_computation.146 | loop fusion | flops 256 | bytes 264 | tf_op jit(solution)/shard_map/mul | solution.py:52
  12.4 5.4 %collective-permute-done = bf16[1,2,32768]{2,1,0:T(2,128)(2,1)S(1)} collective-permute-done((bf16[1,2,32768]{2,1,0:T(2,128)(2,1)}, bf16[1,2,32768]{2,1,0:T(2,128)(2,1)S(1)}, u32[]{:S(2)}, u32[]{:S(2)}) %collective-permute-start) | collective-permute-done | bytes 131104 | tf_op jit(solution)/shard_map/ppermute | solution.py:14
  17.9 4.9 %collective-permute-start.3 = (bf16[1,2,32768]{2,1,0:T(2,128)(2,1)S(1)}, bf16[1,2,32768]{2,1,0:T(2,128)(2,1)S(1)}, u32[]{:S(2)}, u32[]{:S(2)}) collective-permute-start(bf16[1,2,32768]{2,1,0:T(2,128)(2,1)S(1)} %collective-permute-done), channel_id=1, source_target_pairs={{0,4},{1,5},{2,6},{3,7},{4,0},{5,1},{6,2},{7,3},{8,12},{9,13},{10,... | collective-permute-start | bytes 393224 | tf_op jit(solution)/shard_map/ppermute | solution.py:20
  22.8 3.2 %collective-permute-start.2 = (bf16[1,2,32768]{2,1,0:T(2,128)(2,1)S(1)}, bf16[1,2,32768]{2,1,0:T(2,128)(2,1)S(1)}, u32[]{:S(2)}, u32[]{:S(2)}) collective-permute-start(bf16[1,2,32768]{2,1,0:T(2,128)(2,1)S(1)} %collective-permute-done), channel_id=1, source_target_pairs={{0,2},{1,3},{2,0},{3,1},{4,6},{5,7},{6,4},{7,5},{8,10},{9,11},{10,... | collective-permute-start | bytes 393224 | tf_op jit(solution)/shard_map/ppermute | solution.py:20
  26.0 4.7 %collective-permute-start.1 = (bf16[1,2,32768]{2,1,0:T(2,128)(2,1)S(1)}, bf16[1,2,32768]{2,1,0:T(2,128)(2,1)S(1)}, u32[]{:S(2)}, u32[]{:S(2)}) collective-permute-start(bf16[1,2,32768]{2,1,0:T(2,128)(2,1)S(1)} %collective-permute-done), channel_id=1, source_target_pairs={{0,1},{1,0},{2,3},{3,2},{4,5},{5,4},{6,7},{7,6},{8,9},{9,8},{10,11... | collective-permute-start | bytes 393224 | tf_op jit(solution)/shard_map/ppermute | solution.py:20
  31.0 2.2 %collective-permute-done.1 = bf16[1,2,32768]{2,1,0:T(2,128)(2,1)S(1)} collective-permute-done((bf16[1,2,32768]{2,1,0:T(2,128)(2,1)S(1)}, bf16[1,2,32768]{2,1,0:T(2,128)(2,1)S(1)}, u32[]{:S(2)}, u32[]{:S(2)}) %collective-permute-start.1) | collective-permute-done | bytes 131104 | tf_op jit(solution)/shard_map/ppermute | solution.py:20
  33.2 2.7 %convert_reduce_fusion.3 = (bf16[32768]{0:T(1024)(128)(2,1)S(1)}, bf16[32768]{0:T(1024)(128)(2,1)S(1)}, bf16[32768]{0:T(1024)(128)(2,1)S(1)}, bf16[32768]{0:T(10...) fusion(bf16[1,1,2,32768]{3,2,1,0:T(2,128)(2,1)S(1)} %bitcast.229, ...), kind=kLoop, calls=%fused_computation.105 | loop fusion | flops 1048576 | bytes 917504 | tf_op jit(solution)/shard_map/convert.13
  41.6 0.4 convert_element_type.336
  44.4 0.9 subtract_negate_fusion.1
  45.6 2.3 %collective-permute-start.5 = (bf16[1,2,32768]{2,1,0:T(2,128)(2,1)S(1)}, bf16[1,2,32768]{2,1,0:T(2,128)(2,1)S(1)}, u32[]{:S(2)}, u32[]{:S(2)}) collective-permute-start(bf16[1,2,32768]{2,1,0:T(2,128)(2,1)S(1)} %pad_maximum_fusion.1), channel_id=1, source_target_pairs={{0,2},{1,3},{2,0},{3,1},{4,6},{5,7},{6,4},{7,5},{8,10},{9,11},{10,... | collective-permute-start | bytes 393224 | tf_op jit(solution)/shard_map/ppermute | solution.py:20
  49.2 0.4 convert_element_type.354
  50.1 0.9 subtract_negate_fusion
  51.3 1.9 %collective-permute-start.6 = (bf16[1,2,32768]{2,1,0:T(2,128)(2,1)S(1)}, bf16[1,2,32768]{2,1,0:T(2,128)(2,1)S(1)}, u32[]{:S(2)}, u32[]{:S(2)}) collective-permute-start(bf16[1,2,32768]{2,1,0:T(2,128)(2,1)S(1)} %pad_maximum_fusion.2), channel_id=1, source_target_pairs={{0,4},{1,5},{2,6},{3,7},{4,0},{5,1},{6,2},{7,3},{8,12},{9,13},{10,... | collective-permute-start | bytes 393224 | tf_op jit(solution)/shard_map/ppermute | solution.py:20
  54.5 0.4 convert_element_type.328
  55.4 0.9 subtract_negate_fusion.2
  56.6 4.7 %collective-permute-start.4 = (bf16[1,2,32768]{2,1,0:T(2,128)(2,1)S(1)}, bf16[1,2,32768]{2,1,0:T(2,128)(2,1)S(1)}, u32[]{:S(2)}, u32[]{:S(2)}) collective-permute-start(bf16[1,2,32768]{2,1,0:T(2,128)(2,1)S(1)} %pad_maximum_fusion), channel_id=1, source_target_pairs={{0,1},{1,0},{2,3},{3,2},{4,5},{5,4},{6,7},{7,6},{8,9},{9,8},{10,11... | collective-permute-start | bytes 393224 | tf_op jit(solution)/shard_map/ppermute | solution.py:20
  61.3 2.5 %collective-permute-done.4 = bf16[1,2,32768]{2,1,0:T(2,128)(2,1)S(1)} collective-permute-done((bf16[1,2,32768]{2,1,0:T(2,128)(2,1)S(1)}, bf16[1,2,32768]{2,1,0:T(2,128)(2,1)S(1)}, u32[]{:S(2)}, u32[]{:S(2)}) %collective-permute-start.4) | collective-permute-done | bytes 131104 | tf_op jit(solution)/shard_map/ppermute | solution.py:20
  64.0 12.7 %collective-permute-start.7 = (f32[1,2,32768]{2,1,0:T(2,128)S(1)}, f32[1,2,32768]{2,1,0:T(2,128)S(1)}, u32[]{:S(2)}, u32[]{:S(2)}) collective-permute-start(f32[1,2,32768]{2,1,0:T(2,128)S(1)} %convert_add_fusion), channel_id=1, source_target_pairs={{0,576},{16,592},{32,608},{48,624},{64,640},{80,656},{96,672},{112... | collective-permute-start | bytes 786440 | tf_op jit(solution)/shard_map/ppermute | solution.py:14
  76.7 15.3 %collective-permute-done.7 = f32[1,2,32768]{2,1,0:T(2,128)S(1)} collective-permute-done((f32[1,2,32768]{2,1,0:T(2,128)S(1)}, f32[1,2,32768]{2,1,0:T(2,128)S(1)}, u32[]{:S(2)}, u32[]{:S(2)}) %collective-permute-start.7) | collective-permute-done | bytes 262176 | tf_op jit(solution)/shard_map/ppermute | solution.py:14
  92.0 1.4 %fusion.37 = f32[1,1,2,32768]{3,2,1,0:T(2,128)} fusion(f32[1,2,32768]{2,1,0:T(2,128)S(1)} %collective-permute-done.7, f32[1,1,32768]{2,1,0:T(1,128)S(1)} %get-tuple-element.18, f32[1,1,32768]{2,1,0:T(1,128)S(1)} %get-tuple-element.17, f32[1,1,32768]{2,1,0:T(1,128)S(1)} %get-tuple-element.16, f32[1,1,32768]{2,1,0:T(1,128)S(1)} %get-tuple-element.15, ...), kind=kLoop, calls=%fused_computation.58 | loop fusion | flops 393216 | bytes 1310720 | tf_op jit(solution)/shard_map/broadcast_in_dim | solution.py:132
  (66 shorter events, 13.6 us)
Async XLA Ops:
  0.0 17.9 %collective-permute-start = (bf16[1,2,32768]{2,1,0:T(2,128)(2,1)}, bf16[1,2,32768]{2,1,0:T(2,128)(2,1)S(1)}, u32[]{:S(2)}, u32[]{:S(2)}) collective-permute-start(bf16[1,2,32768]{2,1,0:T(2,128)(2,1)} %bitcast.223), channel_id=1, source_target_pairs={{0,192},{16,208},{32,224},{48,240},{64,256},{80,272},{96,288},{112... | collective-permute-start | bytes 393224 | tf_op jit(solution)/shard_map/ppermute | solution.py:14
  8.5 0.7 copy-start.1
  17.9 13.1 %collective-permute-start.3 = (bf16[1,2,32768]{2,1,0:T(2,128)(2,1)S(1)}, bf16[1,2,32768]{2,1,0:T(2,128)(2,1)S(1)}, u32[]{:S(2)}, u32[]{:S(2)}) collective-permute-start(bf16[1,2,32768]{2,1,0:T(2,128)(2,1)S(1)} %collective-permute-done), channel_id=1, source_target_pairs={{0,4},{1,5},{2,6},{3,7},{4,0},{5,1},{6,2},{7,3},{8,12},{9,13},{10,... | collective-permute-start | bytes 393224 | tf_op jit(solution)/shard_map/ppermute | solution.py:20
  22.8 8.2 %collective-permute-start.2 = (bf16[1,2,32768]{2,1,0:T(2,128)(2,1)S(1)}, bf16[1,2,32768]{2,1,0:T(2,128)(2,1)S(1)}, u32[]{:S(2)}, u32[]{:S(2)}) collective-permute-start(bf16[1,2,32768]{2,1,0:T(2,128)(2,1)S(1)} %collective-permute-done), channel_id=1, source_target_pairs={{0,2},{1,3},{2,0},{3,1},{4,6},{5,7},{6,4},{7,5},{8,10},{9,11},{10,... | collective-permute-start | bytes 393224 | tf_op jit(solution)/shard_map/ppermute | solution.py:20
  26.0 7.2 %collective-permute-start.1 = (bf16[1,2,32768]{2,1,0:T(2,128)(2,1)S(1)}, bf16[1,2,32768]{2,1,0:T(2,128)(2,1)S(1)}, u32[]{:S(2)}, u32[]{:S(2)}) collective-permute-start(bf16[1,2,32768]{2,1,0:T(2,128)(2,1)S(1)} %collective-permute-done), channel_id=1, source_target_pairs={{0,1},{1,0},{2,3},{3,2},{4,5},{5,4},{6,7},{7,6},{8,9},{9,8},{10,11... | collective-permute-start | bytes 393224 | tf_op jit(solution)/shard_map/ppermute | solution.py:20
  30.7 2.5 %copy-start = (bf16[1,1,2,32768]{3,2,1,0:T(2,128)(2,1)S(1)}, bf16[1,1,2,32768]{3,2,1,0:T(2,128)(2,1)}, u32[]{:S(2)}) copy-start(bf16[1,1,2,32768]{3,2,1,0:T(2,128)(2,1)} %param.2) | copy-start | bytes 393220
  45.6 15.7 %collective-permute-start.5 = (bf16[1,2,32768]{2,1,0:T(2,128)(2,1)S(1)}, bf16[1,2,32768]{2,1,0:T(2,128)(2,1)S(1)}, u32[]{:S(2)}, u32[]{:S(2)}) collective-permute-start(bf16[1,2,32768]{2,1,0:T(2,128)(2,1)S(1)} %pad_maximum_fusion.1), channel_id=1, source_target_pairs={{0,2},{1,3},{2,0},{3,1},{4,6},{5,7},{6,4},{7,5},{8,10},{9,11},{10,... | collective-permute-start | bytes 393224 | tf_op jit(solution)/shard_map/ppermute | solution.py:20
  51.3 10.0 %collective-permute-start.6 = (bf16[1,2,32768]{2,1,0:T(2,128)(2,1)S(1)}, bf16[1,2,32768]{2,1,0:T(2,128)(2,1)S(1)}, u32[]{:S(2)}, u32[]{:S(2)}) collective-permute-start(bf16[1,2,32768]{2,1,0:T(2,128)(2,1)S(1)} %pad_maximum_fusion.2), channel_id=1, source_target_pairs={{0,4},{1,5},{2,6},{3,7},{4,0},{5,1},{6,2},{7,3},{8,12},{9,13},{10,... | collective-permute-start | bytes 393224 | tf_op jit(solution)/shard_map/ppermute | solution.py:20
  56.6 7.2 %collective-permute-start.4 = (bf16[1,2,32768]{2,1,0:T(2,128)(2,1)S(1)}, bf16[1,2,32768]{2,1,0:T(2,128)(2,1)S(1)}, u32[]{:S(2)}, u32[]{:S(2)}) collective-permute-start(bf16[1,2,32768]{2,1,0:T(2,128)(2,1)S(1)} %pad_maximum_fusion), channel_id=1, source_target_pairs={{0,1},{1,0},{2,3},{3,2},{4,5},{5,4},{6,7},{7,6},{8,9},{9,8},{10,11... | collective-permute-start | bytes 393224 | tf_op jit(solution)/shard_map/ppermute | solution.py:20
  64.0 28.0 %collective-permute-start.7 = (f32[1,2,32768]{2,1,0:T(2,128)S(1)}, f32[1,2,32768]{2,1,0:T(2,128)S(1)}, u32[]{:S(2)}, u32[]{:S(2)}) collective-permute-start(f32[1,2,32768]{2,1,0:T(2,128)S(1)} %convert_add_fusion), channel_id=1, source_target_pairs={{0,576},{16,592},{32,608},{48,624},{64,640},{80,656},{96,672},{112... | collective-permute-start | bytes 786440 | tf_op jit(solution)/shard_map/ppermute | solution.py:14
where the time goes:
time: 93.7 us; the launch traced here: 93.4 us
  starting transfers between devices  42.8 us (46%)
  waiting for transfers between devices  25.4 us (27%)
  other arithmetic  10.2 us (11%)
  local copies, waits for them, and re-layouts  9.35 us (10%)
  matrix products  5.16 us (6%)
    ppermute x6, starting transfers between devices, partner(): return lax.ppermute(value, axis, pairs)  21.6 us
    ppermute x2, starting transfers between devices, shifted(): return lax.ppermute(value, axis, pairs)  21.2 us
    ppermute x2, waiting for transfers between devices, shifted(): return lax.ppermute(value, axis, pairs)  20.7 us
    dot_general x18, matrix products, one_pass(): jnp.einsum('pcme,dcfe->pdfm', shaped, table, preferred_element_type=jnp.f...  4.92 us
    ppermute x6, waiting for transfers between devices, partner(): return lax.ppermute(value, axis, pairs)  4.71 us
    another operation x4, other arithmetic  2.97 us
    neg x3, other arithmetic, apply_fields(): real = -jnp.sum(l_real * w_real - l_imag * w_imag, axis=-2)  2.65 us
    convert_element_type x6, local copies, waits for them, and re-layouts, transform(): second = one_pass(first, table, grid).astype(jnp.bfloat16)  2.21 us
  transfers between devices with their start and end apart: 8, of which 4 were waited for; matrix products, arithmetic and copies ran while one was open for 11% of the time, Pallas kernels for 0%

commit v1 on v0

v1 whole, which is shorter than its diff:
```python
import functools
import math

import jax
import jax.numpy as jnp
import numpy as np
from jax import lax
from jax.experimental import pallas as pl
from jax.experimental.pallas import tpu as pltpu
from jax.sharding import PartitionSpec as P

GRID = 32
ROWS = 256
LANES = 128
CHUNKS = 8
PART = ROWS // CHUNKS
MATCHES = 3
MESH = pl.DeviceIdType.MESH
F32 = jnp.float32
BF16 = jnp.bfloat16


def waves():
    row = np.arange(ROWS)
    lane = np.arange(LANES)
    row_phase = (np.outer(row // 8, row // 8) + 4 * np.outer(row % 8, row % 8)) % GRID
    lane_phase = (8 * np.outer(lane // GRID, lane // GRID) + np.outer(lane % GRID, lane % GRID)) % GRID
    tables = []
    for sign in (1.0, -1.0):
        cosine, sine = (f(row_phase * (2.0 * math.pi / GRID)) for f in (np.cos, np.sin))
        sine = sign * sine
        tables.append(np.block([[cosine, sine], [-sine, cosine]]))
        cosine, sine = (f(lane_phase * (2.0 * math.pi / GRID)) for f in (np.cos, np.sin))
        sine = sign * sine
        tables.append(np.block([[cosine, -sine], [sine, cosine]]))
    return [jnp.asarray(table.astype(np.float32)).astype(BF16) for table in tables]


def part(chunk):
    return pl.ds(chunk * PART, PART)


def signed(index):
    return jnp.where(index < GRID // 2, index, index - GRID).astype(F32)


def coulomb(q, flipped):
    row = lax.broadcasted_iota(jnp.int32, (ROWS, LANES), 0)
    lane = lax.broadcasted_iota(jnp.int32, (ROWS, LANES), 1)
    indices = (row // 8, row % 8 + 8 * (lane // GRID), lane % GRID)
    square = jnp.zeros((ROWS, LANES), F32)
    for index, offset in zip(indices, q):
        if flipped:
            index = (GRID - index) % GRID
        along = signed(index) + offset
        square = square + along * along
    return (32.0 / GRID**3) / (square + 0.25)


def kernel(kpoints, u_ref, coords_ref, rows_f, lanes_f, rows_i, lanes_i, out_ref,
           tab_rf, tab_lf, tab_ri, tab_li, far, near, field, kern, xs, zs, ys,
           tab_sem, far_send, far_recv, near_send, near_recv):
    steps = kpoints // 4
    ka = lax.axis_index("ka")
    ba = lax.axis_index("ba")
    above = lax.rem(ka + steps, kpoints)
    below = lax.rem(ka + kpoints - steps, kpoints)
    bit0 = lax.rem(ba, 2)
    bit1 = lax.rem(ba // 2, 2)
    bit2 = lax.rem(ba // 4, 2)
    partners = (ba + 1 - 2 * bit0, ba + 2 - 4 * bit1, ba + 4 - 8 * bit2)

    loads = []
    for n, (source, target) in enumerate(((rows_f, tab_rf), (lanes_f, tab_lf), (lanes_i, tab_li), (rows_i, tab_ri))):
        loads.append(pltpu.make_async_copy(source, target, tab_sem.at[n]))
        loads[-1].start()

    barrier = pltpu.get_barrier_semaphore()
    for k in (above, below):
        pl.semaphore_signal(barrier, inc=1, device_id=(k, ba), device_id_type=MESH)
    for b in partners:
        pl.semaphore_signal(barrier, inc=1, device_id=(ka, b), device_id_type=MESH)
    pl.semaphore_wait(barrier, 2 + MATCHES)

    def far_copy(way, chunk):
        return pltpu.make_async_remote_copy(
            src_ref=u_ref.at[:, part(chunk)], dst_ref=far.at[way, :, part(chunk)],
            send_sem=far_send.at[way, chunk], recv_sem=far_recv.at[way, chunk],
            device_id=((above, below)[way], ba), device_id_type=MESH)

    def near_copy(way, match, chunk):
        return pltpu.make_async_remote_copy(
            src_ref=far.at[way, :, part(chunk)], dst_ref=near.at[way, match, :, part(chunk)],
            send_sem=near_send.at[way, match, chunk], recv_sem=near_recv.at[way, match, chunk],
            device_id=(ka, partners[match]), device_id_type=MESH)

    for chunk in range(CHUNKS):
        for way in range(2):
            far_copy(way, chunk).start()

    def coord(k, axis):
        return coords_ref[axis, k].astype(F32)

    kern[0] = coulomb([(coord(ka, a) - coord(below, a)) * 0.25 for a in range(3)], False)
    kern[1] = coulomb([(coord(above, a) - coord(ka, a)) * 0.25 for a in range(3)], True)
    f1 = lax.broadcasted_iota(jnp.int32, (PART, LANES), 0) % 8
    y_lo = lax.broadcasted_iota(jnp.int32, (PART, LANES), 1) // GRID
    angle = (f1 * y_lo).astype(F32) * (2.0 * math.pi / GRID)
    tw_cos, tw_sin = jnp.cos(angle), jnp.sin(angle)

    for chunk in range(CHUNKS):
        for way in range(2):
            far_copy(way, chunk).wait_recv()
            for match in range(MATCHES):
                near_copy(way, match, chunk).start()

    for load in loads:
        load.wait()

    def edge(way, match, first):
        v = near.at[way, match]
        for c in range(CHUNKS):
            ur, ui = u_ref[0, part(c)].astype(F32), u_ref[1, part(c)].astype(F32)
            vr, vi = v[0, part(c)].astype(F32), v[1, part(c)].astype(F32)
            xs[part(c), :] = (ur * vr + ui * vi).astype(BF16)
            xs[pl.ds(ROWS + c * PART, PART), :] = (ui * vr - ur * vi).astype(BF16)
        zs[...] = jnp.dot(tab_rf[...], xs[...], preferred_element_type=F32)
        for c in range(CHUNKS):
            zr, zi = zs[part(c), :], zs[pl.ds(ROWS + c * PART, PART), :]
            ys[part(c), :LANES] = (zr * tw_cos + zi * tw_sin).astype(BF16)
            ys[part(c), LANES:] = (zi * tw_cos - zr * tw_sin).astype(BF16)
        field[...] = jnp.dot(ys[...], tab_lf[...], preferred_element_type=F32)
        for c in range(CHUNKS):
            scale = kern[way, part(c), :]
            ys[part(c), :LANES] = (field[part(c), :LANES] * scale).astype(BF16)
            ys[part(c), LANES:] = (field[part(c), LANES:] * scale).astype(BF16)
        field[...] = jnp.dot(ys[...], tab_li[...], preferred_element_type=F32)
        for c in range(CHUNKS):
            fr, fi = field[part(c), :LANES], field[part(c), LANES:]
            xs[part(c), :] = (fr * tw_cos - fi * tw_sin).astype(BF16)
            xs[pl.ds(ROWS + c * PART, PART), :] = (fi * tw_cos + fr * tw_sin).astype(BF16)
        zs[...] = jnp.dot(tab_ri[...], xs[...], preferred_element_type=F32)
        for c in range(CHUNKS):
            vr, vi = v[0, part(c)].astype(F32), v[1, part(c)].astype(F32)
            wr, wi = zs[part(c), :], zs[pl.ds(ROWS + c * PART, PART), :]
            real, imag = vi * wi - vr * wr, -(vr * wi + vi * wr)
            if not first:
                real = out_ref[0, part(c), :] + real
                imag = out_ref[1, part(c), :] + imag
            out_ref[0, part(c), :] = real
            out_ref[1, part(c), :] = imag

    first = True
    for way in range(2):
        for match in range(MATCHES):
            for chunk in range(CHUNKS):
                near_copy(way, match, chunk).wait_recv()
            edge(way, match, first)
            first = False

    for chunk in range(CHUNKS):
        for way in range(2):
            far_copy(way, chunk).wait_send()
            for match in range(MATCHES):
                near_copy(way, match, chunk).wait_send()


def per_device(orbitals, kpoint_coords):
    kpoints = lax.axis_size("ka")
    own = orbitals.reshape(2, ROWS, LANES)
    rows_f, lanes_f, rows_i, lanes_i = waves()
    vmem = pl.BlockSpec(memory_space=pltpu.VMEM)
    whole = pl.BlockSpec(memory_space=pl.ANY)
    sems = pltpu.SemaphoreType.DMA
    out = pl.pallas_call(
        functools.partial(kernel, kpoints),
        out_shape=jax.ShapeDtypeStruct((2, ROWS, LANES), F32),
        in_specs=[vmem, pl.BlockSpec(memory_space=pltpu.SMEM), whole, whole, whole, whole],
        out_specs=vmem,
        scratch_shapes=[
            pltpu.VMEM((2 * ROWS, 2 * ROWS), BF16),
            pltpu.VMEM((2 * LANES, 2 * LANES), BF16),
            pltpu.VMEM((2 * ROWS, 2 * ROWS), BF16),
            pltpu.VMEM((2 * LANES, 2 * LANES), BF16),
            pltpu.VMEM((2, 2, ROWS, LANES), BF16),
            pltpu.VMEM((2, MATCHES, 2, ROWS, LANES), BF16),
            pltpu.VMEM((ROWS, 2 * LANES), F32),
            pltpu.VMEM((2, ROWS, LANES), F32),
            pltpu.VMEM((2 * ROWS, LANES), BF16),
            pltpu.VMEM((2 * ROWS, LANES), F32),
            pltpu.VMEM((ROWS, 2 * LANES), BF16),
            sems((4,)),
            sems((2, CHUNKS)),
            sems((2, CHUNKS)),
            sems((2, MATCHES, CHUNKS)),
            sems((2, MATCHES, CHUNKS)),
        ],
        compiler_params=pltpu.CompilerParams(collective_id=0, has_side_effects=True),
    )(own, kpoint_coords.T, rows_f, lanes_f, rows_i, lanes_i)
    return out.reshape(1, 1, 2, GRID**3)


def solution(mesh):
    return jax.shard_map(
        per_device,
        mesh=mesh,
        in_specs=(P("ka", "ba", None, None), P()),
        out_specs=P("ka", "ba", None, None),
        check_vma=False,
    )
```

time: 93.7 us -> 44.4 us (0.47)
  the two profiles are of different devices: /device:TPU:1 before, /device:TPU:64 now
where the time goes in v1:
time: 44.4 us; the launch traced here: 44.2 us
  Pallas kernels  40.8 us (92%)
  local copies, waits for them, and re-layouts  3.39 us (8%)
    pallas_call x1, Pallas kernels, per_device(): pl.pallas_call(functools.partial(kernel, kpoints), out_shape=jax.ShapeDty...  40.8 us
    reshape x1, local copies, waits for them, and re-layouts, per_device(): return out.reshape(1, 1, 2, GRID ** 3)  1.82 us
    unnamed x1, local copies, waits for them, and re-layouts  1.58 us

profile of v1, /device:TPU:64, one launch (start us, length us, event | category | flops | bytes accessed | tf_op | source)
XLA Modules:
  0.0 44.2 jit_solution(688830732443396003)
XLA Ops:
  0.0 1.6 %copy.9 = bf16[1,2,256,128]{3,2,1,0:T(8,128)(2,1)} copy(bf16[1,2,256,128]{3,1,2,0:T(2,128)(2,1)} %bitcast.7) | data formatting | bytes 262144
  1.6 40.8 %shard_map.64 = f32[2,256,128]{2,1,0:T(8,128)} custom-call(bf16[2,256,128]{2,1,0:T(8,128)(2,1)} %bitcast.6, s32[3,48]{1,0:T(4,128)} %bitcast.8, bf16[512,512]{1,0:T(8,128)(2,1)} %constant.13.rows_f, bf16[256,256]{1,0:T(8,128)(2,1)} %constant.14.lanes_f, bf16[512,512]{1,0:T(8,128)(2,1)} %constant.15.rows_i, bf16[256,256]{1,0:T(8,128)(2,1)} %constant.16.lanes_i), custom_call_target="tpu_custom_call" | custom-call | tf_op jit(solution)/shard_map/pallas_call | solution.py:175
  42.4 1.8 %reshape.7 = f32[1,1,2,32768]{3,2,1,0:T(2,128)} reshape(f32[2,256,128]{2,1,0:T(8,128)} %shard_map.64) | data formatting | bytes 524288 | tf_op jit(solution)/shard_map/reshape | solution.py:200

commit v2 on v1

v2 whole, which is shorter than its diff:
```python
import functools
import math

import jax
import jax.numpy as jnp
import numpy as np
from jax import lax
from jax.experimental import pallas as pl
from jax.experimental.pallas import tpu as pltpu
from jax.sharding import PartitionSpec as P

GRID = 32
ROWS = 256
LANES = 128
CHUNKS = 8
COLLECTIVE = 0
VMEM = 24 * 2**20
PART = ROWS // CHUNKS
HOLD = 4
MATCHES = 3
MESH = pl.DeviceIdType.MESH
F32 = jnp.float32
BF16 = jnp.bfloat16


def waves():
    row = np.arange(ROWS)
    lane = np.arange(LANES)
    row_phase = (np.outer(row // 8, row // 8) + 4 * np.outer(row % 8, row % 8)) % GRID
    lane_phase = (8 * np.outer(lane // GRID, lane // GRID) + np.outer(lane % GRID, lane % GRID)) % GRID
    tables = []
    for sign in (1.0, -1.0):
        cosine, sine = (f(row_phase * (2.0 * math.pi / GRID)) for f in (np.cos, np.sin))
        sine = sign * sine
        tables.append(np.block([[cosine, sine], [-sine, cosine]]))
        cosine, sine = (f(lane_phase * (2.0 * math.pi / GRID)) for f in (np.cos, np.sin))
        sine = sign * sine
        tables.append(np.block([[cosine, -sine], [sine, cosine]]))
    angle = np.outer(np.arange(PART) % 8, lane // GRID) * (2.0 * math.pi / GRID)
    turn = jnp.asarray(np.stack([np.cos(angle), np.sin(angle)]).astype(np.float32))
    return [jnp.asarray(table.astype(np.float32)).astype(BF16) for table in tables] + [turn]


def part(chunk):
    return pl.ds(chunk * PART, PART)


def pairs(chunk):
    return pl.ds(chunk * 2 * PART, 2 * PART)


def reals(chunk):
    return pl.ds(chunk * 2 * PART, PART, stride=2)


def imags(chunk):
    return pl.ds(chunk * 2 * PART + 1, PART, stride=2)


def signed(index):
    return jnp.where(index < GRID // 2, index, index - GRID).astype(F32)


def coulomb(q, flipped):
    row = lax.broadcasted_iota(jnp.int32, (ROWS, LANES), 0)
    lane = lax.broadcasted_iota(jnp.int32, (ROWS, LANES), 1)
    indices = (row // 8, row % 8 + 8 * (lane // GRID), lane % GRID)
    square = jnp.zeros((ROWS, LANES), F32)
    for index, offset in zip(indices, q):
        if flipped:
            index = (GRID - index) % GRID
        along = signed(index) + offset
        square = square + along * along
    return (32.0 / GRID**3) / (square + 0.25)


def kernel(kpoints, u_hbm, coords_hbm, rows_f, lanes_f, rows_i, lanes_i, turn, out_ref,
           tab_rf, tab_lf, tab_li, tab_ri, tab_turn, coords, u_raw, far, near, own, raw, total, kern, xs, zs, ys, fs,
           tab_sem, far_send, far_recv, near_send, near_recv, ready):
    steps = kpoints // 4
    ka = lax.axis_index("ka")
    ba = lax.axis_index("ba")
    quarter = ka // steps
    first = lax.rem(quarter + 3, 4) // 2
    last = 1 - first
    bit0 = lax.rem(ba, 2)
    bit1 = lax.rem(ba // 2, 2)
    bit2 = lax.rem(ba // 4, 2)
    partners = (ba + 1 - 2 * bit0, ba + 2 - 4 * bit1, ba + 4 - 8 * bit2)

    def beside(side):
        return lax.rem(ka + kpoints + (2 * side - 1) * steps, kpoints)

    loads = []
    for n, (source, target) in enumerate(((u_hbm, u_raw), (coords_hbm, coords), (turn, tab_turn), (rows_f, tab_rf),
                                          (lanes_f, tab_lf), (lanes_i, tab_li), (rows_i, tab_ri))):
        loads.append(pltpu.make_async_copy(source, target, tab_sem.at[n]))

    def signal(semaphore, k, b):
        pl.semaphore_signal(semaphore, inc=1, device_id=(k, b), device_id_type=MESH)

    barrier = pltpu.get_barrier_semaphore()

    @pl.when(quarter == 0)
    def _():
        signal(barrier, beside(first), ba)

    @pl.when(quarter != 3)
    def _():
        signal(barrier, beside(last), ba)

    for b in partners:
        signal(barrier, ka, b)
    for load in loads:
        load.start()
    pl.semaphore_wait(barrier, MATCHES + (quarter + 2) // 3 + quarter // 3)

    @pl.when(quarter != 0)
    def _():
        signal(ready.at[quarter // 2], beside(first), ba)

    @pl.when(quarter == 3)
    def _():
        signal(ready.at[1], beside(last), ba)

    def far_copy(side, chunk):
        return pltpu.make_async_remote_copy(
            src_ref=u_hbm.at[pairs(chunk)], dst_ref=far.at[1 - side, pairs(chunk)],
            send_sem=far_send.at[side, chunk], recv_sem=far_recv.at[1 - side, chunk],
            device_id=(beside(side), ba), device_id_type=MESH)

    def far_arrived(side, chunk):
        pltpu.make_async_remote_copy(
            src_ref=u_hbm.at[pairs(chunk)], dst_ref=far.at[side, pairs(chunk)],
            send_sem=far_send.at[side, chunk], recv_sem=far_recv.at[side, chunk],
            device_id=(beside(side), ba), device_id_type=MESH).wait_recv()

    def near_copy(side, match, chunk):
        return pltpu.make_async_remote_copy(
            src_ref=far.at[side, pairs(chunk)], dst_ref=near.at[side, match, pairs(chunk)],
            send_sem=near_send.at[side, match, chunk], recv_sem=near_recv.at[side, match, chunk],
            device_id=(ka, partners[match]), device_id_type=MESH)

    def send(side):
        for chunk in range(CHUNKS):
            far_copy(side, chunk).start()

    def forward(side, chunk):
        far_arrived(side, chunk)
        for match in reversed(range(MATCHES)):
            near_copy(side, match, chunk).start()

    @pl.when(quarter == 0)
    def _():
        pl.semaphore_wait(ready.at[0], 1)

    send(first)

    @pl.when(quarter == 2)
    def _():
        pl.semaphore_wait(ready.at[1], 1)

    @pl.when(quarter >= 2)
    def _():
        send(last)

    loads[1].wait()

    def coord(k, axis):
        return coords[axis, k].astype(F32)

    below, above = beside(0), beside(1)
    kern[0] = coulomb([(coord(ka, a) - coord(below, a)) * 0.25 for a in range(3)], False)
    kern[1] = coulomb([(coord(above, a) - coord(ka, a)) * 0.25 for a in range(3)], True)
    loads[0].wait()
    for c in range(CHUNKS):
        raw[0, pairs(c), :] = u_raw[pairs(c), :].astype(F32)
    for c in range(CHUNKS):
        own[0, part(c), :] = raw[0, reals(c), :]
        own[1, part(c), :] = raw[0, imags(c), :]
    for load in loads[2:]:
        load.wait()

    for chunk in range(HOLD):
        forward(first, chunk)

    @pl.when(quarter < 2)
    def _():
        pl.semaphore_wait(ready.at[1], 1)
        send(last)

    for chunk in range(HOLD, CHUNKS):
        forward(first, chunk)

    def lanes(match):
        return pl.ds(match * LANES, LANES)

    def rows(match, c):
        return pl.ds(match * ROWS + c * PART, PART)

    def densities(side):
        for match in range(MATCHES):
            for chunk in range(CHUNKS):
                near_copy(side, match, chunk).wait_recv()
            for c in range(CHUNKS):
                raw[match, pairs(c), :] = near[side, match, pairs(c), :].astype(F32)
            for c in range(CHUNKS):
                ur, ui = own[0, part(c), :], own[1, part(c), :]
                vr, vi = raw[match, reals(c), :], raw[match, imags(c), :]
                xs[part(c), lanes(match)] = (ur * vr + ui * vi).astype(BF16)
                xs[part(CHUNKS + c), lanes(match)] = (ui * vr - ur * vi).astype(BF16)

    def turn_in():
        for match in range(MATCHES):
            for c in range(CHUNKS):
                zr, zi = zs[part(c), lanes(match)], zs[part(CHUNKS + c), lanes(match)]
                ys[rows(match, c), :LANES] = (zr * tab_turn[0] + zi * tab_turn[1]).astype(BF16)
                ys[rows(match, c), LANES:] = (zi * tab_turn[0] - zr * tab_turn[1]).astype(BF16)

    def screen(side):
        for match in range(MATCHES):
            for c in range(CHUNKS):
                scale = kern[side, part(c), :]
                ys[rows(match, c), :LANES] = (fs[rows(match, c), :LANES] * scale).astype(BF16)
                ys[rows(match, c), LANES:] = (fs[rows(match, c), LANES:] * scale).astype(BF16)

    def turn_back():
        for match in range(MATCHES):
            for c in range(CHUNKS):
                fr, fi = fs[rows(match, c), :LANES], fs[rows(match, c), LANES:]
                xs[part(c), lanes(match)] = (fr * tab_turn[0] - fi * tab_turn[1]).astype(BF16)
                xs[part(CHUNKS + c), lanes(match)] = (fi * tab_turn[0] + fr * tab_turn[1]).astype(BF16)

    def product(target, left, right):
        target[...] = jnp.dot(left[...], right[...], preferred_element_type=F32)

    def apply(final):
        for c in range(CHUNKS):
            real = total[0, part(c), :] if final else jnp.zeros((PART, LANES), F32)
            imag = total[1, part(c), :] if final else jnp.zeros((PART, LANES), F32)
            for match in range(MATCHES):
                vr, vi = raw[match, reals(c), :], raw[match, imags(c), :]
                wr, wi = zs[part(c), lanes(match)], zs[part(CHUNKS + c), lanes(match)]
                real = real + (vi * wi - vr * wr)
                imag = imag - (vr * wi + vi * wr)
            if final:
                out_ref[reals(c), :] = real
                out_ref[imags(c), :] = imag
            else:
                total[0, part(c), :] = real
                total[1, part(c), :] = imag

    def stages(side, final):
        return (
            lambda: densities(side),
            lambda: product(zs, tab_rf, xs),
            turn_in,
            lambda: product(fs, ys, tab_lf),
            lambda: screen(side),
            lambda: product(fs, ys, tab_li),
            lambda: (turn_back(), product(zs, tab_ri, xs)),
            lambda: apply(final),
        )

    for chunk, stage in enumerate(stages(first, False)):
        forward(last, chunk)
        stage()
    for stage in stages(last, True):
        stage()

    for side in range(2):
        for chunk in range(CHUNKS):
            far_copy(side, chunk).wait_send()
            for match in range(MATCHES):
                near_copy(side, match, chunk).wait_send()


def per_device(orbitals, kpoint_coords):
    kpoints = lax.axis_size("ka")
    own = orbitals.reshape(2, ROWS, LANES).transpose(1, 0, 2).reshape(2 * ROWS, LANES)
    whole = pl.BlockSpec(memory_space=pltpu.HBM)
    sems = pltpu.SemaphoreType.DMA
    tables = waves()
    out = pl.pallas_call(
        functools.partial(kernel, kpoints),
        out_shape=jax.ShapeDtypeStruct((2 * ROWS, LANES), F32),
        in_specs=[whole] * (2 + len(tables)),
        out_specs=pl.BlockSpec(memory_space=pltpu.VMEM),
        scratch_shapes=[
            pltpu.VMEM((2 * ROWS, 2 * ROWS), BF16),
            pltpu.VMEM((2 * LANES, 2 * LANES), BF16),
            pltpu.VMEM((2 * LANES, 2 * LANES), BF16),
            pltpu.VMEM((2 * ROWS, 2 * ROWS), BF16),
            pltpu.VMEM((2, PART, LANES), F32),
            pltpu.SMEM((3, kpoints), jnp.int32),
            pltpu.VMEM((2 * ROWS, LANES), BF16),
            pltpu.VMEM((2, 2 * ROWS, LANES), BF16),
            pltpu.VMEM((2, MATCHES, 2 * ROWS, LANES), BF16),
            pltpu.VMEM((2, ROWS, LANES), F32),
            pltpu.VMEM((MATCHES, 2 * ROWS, LANES), F32),
            pltpu.VMEM((2, ROWS, LANES), F32),
            pltpu.VMEM((2, ROWS, LANES), F32),
            pltpu.VMEM((2 * ROWS, MATCHES * LANES), BF16),
            pltpu.VMEM((2 * ROWS, MATCHES * LANES), F32),
            pltpu.VMEM((MATCHES * ROWS, 2 * LANES), BF16),
            pltpu.VMEM((MATCHES * ROWS, 2 * LANES), F32),
            sems((7,)),
            sems((2, CHUNKS)),
            sems((2, CHUNKS)),
            sems((2, MATCHES, CHUNKS)),
            sems((2, MATCHES, CHUNKS)),
            pltpu.SemaphoreType.REGULAR((2,)),
        ],
        compiler_params=pltpu.CompilerParams(collective_id=COLLECTIVE, has_side_effects=True, vmem_limit_bytes=VMEM),
    )(*(pltpu.with_memory_space_constraint(a, pltpu.HBM) for a in (own, kpoint_coords.T, *tables)))
    return out.reshape(ROWS, 2, LANES).transpose(1, 0, 2).reshape(1, 1, 2, GRID**3)


def solution(mesh):
    return jax.shard_map(
        per_device,
        mesh=mesh,
        in_specs=(P("ka", "ba", None, None), P()),
        out_specs=P("ka", "ba", None, None),
        check_vma=False,
    )
```

time: 44.4 us -> 39.5 us (0.89)
  the two profiles are of different devices: /device:TPU:64 before, /device:TPU:520 now
where the time goes in v2:
time: 39.5 us; the launch traced here: 39.3 us
  Pallas kernels  38.6 us (98%)
  local copies, waits for them, and re-layouts  0.71 us (2%)
    pallas_call x1, Pallas kernels, per_device(): pl.pallas_call(functools.partial(kernel, kpoints), out_shape=jax.ShapeDty...  38.6 us

profile of v2, /device:TPU:520, one launch (start us, length us, event | category | flops | bytes accessed | tf_op | source)
XLA Modules:
  0.0 39.3 jit_solution(6483865243926598323)
XLA Ops:
  0.0 38.6 %shard_map.73 = f32[512,128]{1,0:T(8,128)S(1)} custom-call(bf16[512,128]{1,0:T(8,128)(2,1)} %bitcast.12, s32[3,48]{1,0:T(4,128)} %bitcast.13, bf16[512,512]{1,0:T(8,128)(2,1)} %constant.16.rows_f, bf16[256,256]{1,0:T(8,128)(2,1)} %constant.17.lanes_f, bf16[512,512]{1,0:T(8,128)(2,1)} %constant.18.rows_i, bf16[256,256]{1,0:T(8,128)(2,1)} %constant.19.lanes_i, ...), custom_call_target="tpu_custom_call" | custom-call | tf_op jit(solution)/shard_map/pallas_call | solution.py:284
  38.6 0.7 %copy.11 = f32[1,1,2,32768]{3,2,1,0:T(2,128)} copy(f32[1,1,2,32768]{3,2,1,0:T(2,128)S(1)} %bitcast.11) | data formatting | bytes 524288

commit v3 on v2

--- a/solution.py
+++ b/solution.py
@@ -15,8 +15,10 @@
 CHUNKS = 8
 COLLECTIVE = 0
 VMEM = 24 * 2**20
-PART = ROWS // CHUNKS
-HOLD = 4
+LEADS = (8, 3, 3, 3)
+HOLDS = (4, 0, 0)
+BLOCKS = 8
+PART = ROWS // BLOCKS
 MATCHES = 3
 MESH = pl.DeviceIdType.MESH
 F32 = jnp.float32
@@ -45,6 +47,10 @@
     return pl.ds(chunk * PART, PART)
 
 
+def piece(chunk):
+    return pl.ds(chunk * (2 * ROWS // CHUNKS), 2 * ROWS // CHUNKS)
+
+
 def pairs(chunk):
     return pl.ds(chunk * 2 * PART, 2 * PART)
 
@@ -125,19 +131,19 @@
 
     def far_copy(side, chunk):
         return pltpu.make_async_remote_copy(
-            src_ref=u_hbm.at[pairs(chunk)], dst_ref=far.at[1 - side, pairs(chunk)],
+            src_ref=u_hbm.at[piece(chunk)], dst_ref=far.at[1 - side, piece(chunk)],
             send_sem=far_send.at[side, chunk], recv_sem=far_recv.at[1 - side, chunk],
             device_id=(beside(side), ba), device_id_type=MESH)
 
     def far_arrived(side, chunk):
         pltpu.make_async_remote_copy(
-            src_ref=u_hbm.at[pairs(chunk)], dst_ref=far.at[side, pairs(chunk)],
+            src_ref=u_hbm.at[piece(chunk)], dst_ref=far.at[side, piece(chunk)],
             send_sem=far_send.at[side, chunk], recv_sem=far_recv.at[side, chunk],
             device_id=(beside(side), ba), device_id_type=MESH).wait_recv()
 
     def near_copy(side, match, chunk):
         return pltpu.make_async_remote_copy(
-            src_ref=far.at[side, pairs(chunk)], dst_ref=near.at[side, match, pairs(chunk)],
+            src_ref=far.at[side, piece(chunk)], dst_ref=near.at[side, match, piece(chunk)],
             send_sem=near_send.at[side, match, chunk], recv_sem=near_recv.at[side, match, chunk],
             device_id=(ka, partners[match]), device_id_type=MESH)
 
@@ -156,11 +162,7 @@
 
     send(first)
 
-    @pl.when(quarter == 2)
-    def _():
-        pl.semaphore_wait(ready.at[1], 1)
-
-    @pl.when(quarter >= 2)
+    @pl.when(quarter == 3)
     def _():
         send(last)
 
@@ -173,24 +175,31 @@
     kern[0] = coulomb([(coord(ka, a) - coord(below, a)) * 0.25 for a in range(3)], False)
     kern[1] = coulomb([(coord(above, a) - coord(ka, a)) * 0.25 for a in range(3)], True)
     loads[0].wait()
-    for c in range(CHUNKS):
+    for c in range(BLOCKS):
         raw[0, pairs(c), :] = u_raw[pairs(c), :].astype(F32)
-    for c in range(CHUNKS):
+    for c in range(BLOCKS):
         own[0, part(c), :] = raw[0, reals(c), :]
         own[1, part(c), :] = raw[0, imags(c), :]
     for load in loads[2:]:
         load.wait()
 
-    for chunk in range(HOLD):
-        forward(first, chunk)
-
-    @pl.when(quarter < 2)
-    def _():
-        pl.semaphore_wait(ready.at[1], 1)
-        send(last)
-
-    for chunk in range(HOLD, CHUNKS):
-        forward(first, chunk)
+    def take(lead, hold):
+        taken = 0
+        for chunk in range(CHUNKS):
+            if chunk == hold:
+                pl.semaphore_wait(ready.at[1], 1)
+                send(last)
+            if chunk >= lead:
+                forward(last, taken)
+                taken += 1
+            forward(first, chunk)
+        for chunk in range(taken, CHUNKS):
+            forward(last, chunk)
+
+    for number, lead in enumerate(LEADS):
+        @pl.when(quarter == number)
+        def _():
+            take(lead, HOLDS[number] if number < 3 else None)
 
     def lanes(match):
         return pl.ds(match * LANES, LANES)
@@ -202,45 +211,45 @@
         for match in range(MATCHES):
             for chunk in range(CHUNKS):
                 near_copy(side, match, chunk).wait_recv()
-            for c in range(CHUNKS):
+            for c in range(BLOCKS):
                 raw[match, pairs(c), :] = near[side, match, pairs(c), :].astype(F32)
-            for c in range(CHUNKS):
+            for c in range(BLOCKS):
                 ur, ui = own[0, part(c), :], own[1, part(c), :]
                 vr, vi = raw[match, reals(c), :], raw[match, imags(c), :]
                 xs[part(c), lanes(match)] = (ur * vr + ui * vi).astype(BF16)
-                xs[part(CHUNKS + c), lanes(match)] = (ui * vr - ur * vi).astype(BF16)
+                xs[part(BLOCKS + c), lanes(match)] = (ui * vr - ur * vi).astype(BF16)
 
     def turn_in():
         for match in range(MATCHES):
-            for c in range(CHUNKS):
-                zr, zi = zs[part(c), lanes(match)], zs[part(CHUNKS + c), lanes(match)]
+            for c in range(BLOCKS):
+                zr, zi = zs[part(c), lanes(match)], zs[part(BLOCKS + c), lanes(match)]
                 ys[rows(match, c), :LANES] = (zr * tab_turn[0] + zi * tab_turn[1]).astype(BF16)
                 ys[rows(match, c), LANES:] = (zi * tab_turn[0] - zr * tab_turn[1]).astype(BF16)
 
     def screen(side):
         for match in range(MATCHES):
-            for c in range(CHUNKS):
+            for c in range(BLOCKS):
                 scale = kern[side, part(c), :]
                 ys[rows(match, c), :LANES] = (fs[rows(match, c), :LANES] * scale).astype(BF16)
                 ys[rows(match, c), LANES:] = (fs[rows(match, c), LANES:] * scale).astype(BF16)
 
     def turn_back():
         for match in range(MATCHES):
-            for c in range(CHUNKS):
+            for c in range(BLOCKS):
                 fr, fi = fs[rows(match, c), :LANES], fs[rows(match, c), LANES:]
                 xs[part(c), lanes(match)] = (fr * tab_turn[0] - fi * tab_turn[1]).astype(BF16)
-                xs[part(CHUNKS + c), lanes(match)] = (fi * tab_turn[0] + fr * tab_turn[1]).astype(BF16)
+                xs[part(BLOCKS + c), lanes(match)] = (fi * tab_turn[0] + fr * tab_turn[1]).astype(BF16)
 
     def product(target, left, right):
         target[...] = jnp.dot(left[...], right[...], preferred_element_type=F32)
 
     def apply(final):
-        for c in range(CHUNKS):
+        for c in range(BLOCKS):
             real = total[0, part(c), :] if final else jnp.zeros((PART, LANES), F32)
             imag = total[1, part(c), :] if final else jnp.zeros((PART, LANES), F32)
             for match in range(MATCHES):
                 vr, vi = raw[match, reals(c), :], raw[match, imags(c), :]
-                wr, wi = zs[part(c), lanes(match)], zs[part(CHUNKS + c), lanes(match)]
+                wr, wi = zs[part(c), lanes(match)], zs[part(BLOCKS + c), lanes(match)]
                 real = real + (vi * wi - vr * wr)
                 imag = imag - (vr * wi + vi * wr)
             if final:
@@ -262,8 +271,7 @@
             lambda: apply(final),
         )
 
-    for chunk, stage in enumerate(stages(first, False)):
-        forward(last, chunk)
+    for stage in stages(first, False):
         stage()
     for stage in stages(last, True):
         stage()

time: 39.5 us -> 33.3 us (0.84)
  the two profiles are of different devices: /device:TPU:520 before, /device:TPU:64 now
where the time goes in v3:
time: 33.3 us; the launch traced here: 33.1 us
  Pallas kernels  32.4 us (97%)
  local copies, waits for them, and re-layouts  0.71 us (2%)
    pallas_call x1, Pallas kernels, per_device(): pl.pallas_call(functools.partial(kernel, kpoints), out_shape=jax.ShapeDty...  32.4 us
    unnamed x1, local copies, waits for them, and re-layouts  0.71 us

profile of v3, /device:TPU:64, one launch (start us, length us, event | category | flops | bytes accessed | tf_op | source)
XLA Modules:
  0.0 33.1 jit_solution(2288427226132613758)
XLA Ops:
  0.0 32.4 %shard_map.73 = f32[512,128]{1,0:T(8,128)S(1)} custom-call(bf16[512,128]{1,0:T(8,128)(2,1)} %bitcast.12, s32[3,48]{1,0:T(4,128)} %bitcast.13, bf16[512,512]{1,0:T(8,128)(2,1)} %constant.16.rows_f, bf16[256,256]{1,0:T(8,128)(2,1)} %constant.17.lanes_f, bf16[512,512]{1,0:T(8,128)(2,1)} %constant.18.rows_i, bf16[256,256]{1,0:T(8,128)(2,1)} %constant.19.lanes_i, ...), custom_call_target="tpu_custom_call" | custom-call | tf_op jit(solution)/shard_map/pallas_call | solution.py:292
  32.4 0.7 %copy.11 = f32[1,1,2,32768]{3,2,1,0:T(2,128)} copy(f32[1,1,2,32768]{3,2,1,0:T(2,128)S(1)} %bitcast.11) | data formatting | bytes 524288
